TPU v7x, 32 devices: a whole 2x2x4 slice. The times are simulated.
32 devices in a mesh: dp: 8 (over z, x), tensor: 4 (over y, core).
Axes of the slice: x: 2, y: 2, z: 4, core: 2. Of those that a mesh axis runs over, the one named last changes fastest.
Arguments:
- layer_input: bfloat16 [8192, 2048], P(('dp', 'tensor')), may hold values from -6 to 6
- segments: int32 [8192], P('dp'), may hold values from 0 to 8191, as said below
- positions: int32 [8192], P('dp'), may hold values from 0 to 1023, as said below
- first_gain: bfloat16 [2048], P('dp'), may hold values from 0.5 to 1.5
- first_shift: bfloat16 [2048], P('dp'), may hold values from -4 to 4
- query_weight: bfloat16 [2048, 2048], P('dp', 'tensor'), may hold values from -0.125 to 0.125
- key_weight: bfloat16 [2048, 2048], P('dp', 'tensor'), may hold values from -0.125 to 0.125
- value_weight: bfloat16 [2048, 2048], P('dp', 'tensor'), may hold values from -0.125 to 0.125
- query_bias: bfloat16 [32, 64], P('tensor', 'dp'), may hold values from -6 to 6
- key_bias: bfloat16 [32, 16], P('tensor'), may hold values from -6 to 6
- value_bias: bfloat16 [32, 64], P('tensor', 'dp'), may hold values from -6 to 6
- out_weight: bfloat16 [2048, 2048], P('tensor', 'dp'), may hold values from -0.5 to 0.5
- second_gain: bfloat16 [2048], P('dp'), may hold values from 0.5 to 1.5
- second_shift: bfloat16 [2048], P('dp'), may hold values from -4 to 4
- gate_weight: bfloat16 [2048, 5632], P('dp', 'tensor'), may hold values from -0.125 to 0.125
- up_weight: bfloat16 [2048, 5632], P('dp', 'tensor'), may hold values from -0.125 to 0.125
- down_weight: bfloat16 [5632, 2048], P('tensor', 'dp'), may hold values from -0.078125 to 0.078125
- out_grad: bfloat16 [8192, 2048], P(('dp', 'tensor')), may hold values from -6 to 6
Outputs:
- layer_output: bfloat16 [8192, 2048], P(('dp', 'tensor'))
- input_grad: float32 [8192, 2048], P(('dp', 'tensor'))
- first_gain_grad: float32 [2048], P(('dp', 'tensor'))
- first_shift_grad: float32 [2048], P(('dp', 'tensor'))
- query_weight_grad: float32 [2048, 2048], P('dp', 'tensor')
- key_weight_grad: float32 [2048, 2048], P('dp', 'tensor')
- value_weight_grad: float32 [2048, 2048], P('dp', 'tensor')
- query_bias_grad: float32 [32, 64], P('tensor', 'dp')
- key_bias_grad: float32 [32, 16], P('tensor')
- value_bias_grad: float32 [32, 64], P('tensor', 'dp')
- out_weight_grad: float32 [2048, 2048], P('tensor', 'dp')
- second_gain_grad: float32 [2048], P(('dp', 'tensor'))
- second_shift_grad: float32 [2048], P(('dp', 'tensor'))
- gate_weight_grad: float32 [2048, 5632], P('dp', 'tensor')
- up_weight_grad: float32 [2048, 5632], P('dp', 'tensor')
- down_weight_grad: float32 [5632, 2048], P('tensor', 'dp')
Inputs may be any that keep to these rules, and one draw needn't show every extreme that they name: `segments`: the tokens form runs of 1024 rows that start at multiples of 1024; the first token of each run starts a new segment. A token's segment number is the row index of the last token of its segment, so numbers never fall along the rows and no two runs share one. `positions`: each token's position counts the earlier tokens of its segment.
All inputs are finite; a program needn't handle non-finite values.
Results may differ from a plain program's by a relative error of at most 0.015.
Values may be sent and summed in bfloat16 or wider, within the bound.
A program may use at most 256 MiB of HBM per device.

v0:
```python
import math
import jax
import jax.numpy as jnp
from jax import lax
from jax.sharding import PartitionSpec as P

HD = 64
ROT = 16
SEQ = 1024
EPS = 1e-05
NEG = -1e30


def rope_angles(positions):
    half = ROT // 2
    freqs = jnp.exp(-(2.0 / ROT) * jnp.arange(half).astype(jnp.float32) * math.log(10000.0))
    return positions.astype(jnp.float32)[:, None] * freqs[None, :]


def turn(heads, cosine, sine, direction):
    half = ROT // 2
    first = heads[..., :half]
    second = heads[..., half:ROT]
    return jnp.concatenate(
        [
            first * cosine - direction * second * sine,
            second * cosine + direction * first * sine,
            heads[..., ROT:],
        ],
        axis=-1,
    )


def norm_forward(rows, gain, shift):
    center = rows - jnp.mean(rows, axis=-1, keepdims=True)
    rstd = lax.rsqrt(jnp.mean(center * center, axis=-1, keepdims=True) + EPS)
    normal = center * rstd
    return (normal, rstd, normal * gain + shift)


def norm_backward(grad_out, normal, rstd, gain):
    scaled = grad_out * gain
    return rstd * (
        scaled
        - jnp.mean(scaled, axis=-1, keepdims=True)
        - normal * jnp.mean(scaled * normal, axis=-1, keepdims=True)
    )


def allowed_pairs(segments, start, base, block):
    q_index = start + jnp.arange(block, dtype=jnp.int32)
    k_index = base + jnp.arange(SEQ, dtype=jnp.int32)
    q_segs = lax.dynamic_slice_in_dim(segments, start, block, 0)
    return (k_index[None, :] <= q_index[:, None]) & (segments[None, :] == q_segs[:, None])


def block_scores(q_rot, k_rot, segments, number, block):
    start = number * block
    base = start // SEQ * SEQ
    q_part = lax.dynamic_slice_in_dim(q_rot, start, block, 0)
    raw = jnp.einsum("qhd,khd->hqk", q_part, k_rot, preferred_element_type=jnp.float32)
    allowed = allowed_pairs(segments, start, base, block)
    scores = jnp.where(allowed[None], raw * HD ** (-0.5), NEG)
    return (scores, start, base, q_part, k_rot)


def attend_forward(q_rot, k_rot, v_heads, segments):
    block = min(512, SEQ)
    count = q_rot.shape[0] // block

    def one_block(number):
        scores, start, base, q_part, k_part = block_scores(q_rot, k_rot, segments, number, block)
        top = jnp.max(scores, axis=-1, keepdims=True)
        expo = jnp.exp(scores - top)
        total = jnp.sum(expo, axis=-1, keepdims=True)
        probs = (expo / total).astype(jnp.bfloat16)
        mixed = jnp.einsum("hqk,khd->qhd", probs, v_heads, preferred_element_type=jnp.float32)
        return (mixed, (top + jnp.log(total))[..., 0])

    mixed, log_sums = lax.map(one_block, jnp.arange(count, dtype=jnp.int32))
    return (mixed.reshape(q_rot.shape), log_sums)


def attend_backward(q_rot, k_rot, v_heads, segments, log_sums, grad_mixed):
    block = min(512, SEQ)
    count = q_rot.shape[0] // block
    start_acc = (jnp.zeros(k_rot.shape, jnp.float32), jnp.zeros(v_heads.shape, jnp.float32))

    def one_block(carry, item):
        key_acc, value_acc = carry
        number, log_part = item
        scores, start, base, q_part, k_part = block_scores(q_rot, k_rot, segments, number, block)
        grad_part = lax.dynamic_slice_in_dim(grad_mixed, start, block, 0)
        probs = jnp.exp(scores - log_part[..., None])
        grad_probs = jnp.einsum(
            "qhd,khd->hqk", grad_part, v_heads, preferred_element_type=jnp.float32
        )
        inner = jnp.sum(probs * grad_probs, axis=-1, keepdims=True)
        grad_scores = (probs * (grad_probs - inner) * HD ** (-0.5)).astype(jnp.bfloat16)
        q_grad = jnp.einsum("hqk,khd->qhd", grad_scores, k_part, preferred_element_type=jnp.float32)
        k_grad = jnp.einsum("hqk,qhd->khd", grad_scores, q_part, preferred_element_type=jnp.float32)
        v_grad = jnp.einsum(
            "hqk,qhd->khd",
            probs.astype(jnp.bfloat16),
            grad_part,
            preferred_element_type=jnp.float32,
        )
        key_acc = key_acc + k_grad
        value_acc = value_acc + v_grad
        return ((key_acc, value_acc), q_grad)

    (key_acc, value_acc), q_blocks = lax.scan(
        one_block, start_acc, (jnp.arange(count, dtype=jnp.int32), log_sums)
    )
    return (q_blocks.reshape(q_rot.shape), key_acc, value_acc)


def local(
    layer_input,
    segments,
    positions,
    first_gain,
    first_shift,
    query_weight,
    key_weight,
    value_weight,
    query_bias,
    key_bias,
    value_bias,
    out_weight,
    second_gain,
    second_shift,
    gate_weight,
    up_weight,
    down_weight,
    out_grad,
):
    f32 = jnp.float32
    bf16 = jnp.bfloat16
    query_full, key_full, value_full, out_full, bias_query, bias_value, gain_one, shift_one = (
        lax.all_gather(query_weight, "dp", axis=0, tiled=True),
        lax.all_gather(key_weight, "dp", axis=0, tiled=True),
        lax.all_gather(value_weight, "dp", axis=0, tiled=True),
        lax.all_gather(out_weight, "dp", axis=1, tiled=True),
        lax.all_gather(query_bias, "dp", axis=1, tiled=True),
        lax.all_gather(value_bias, "dp", axis=1, tiled=True),
        lax.all_gather(first_gain, "dp", axis=0, tiled=True),
        lax.all_gather(first_shift, "dp", axis=0, tiled=True),
    )
    gate_full, up_full, down_full, gain_two, shift_two = (
        lax.all_gather(gate_weight, "dp", axis=0, tiled=True),
        lax.all_gather(up_weight, "dp", axis=0, tiled=True),
        lax.all_gather(down_weight, "dp", axis=1, tiled=True),
        lax.all_gather(second_gain, "dp", axis=0, tiled=True),
        lax.all_gather(second_shift, "dp", axis=0, tiled=True),
    )
    rows = layer_input.astype(f32)
    gain_one_f = gain_one.astype(f32)
    hat_one, rstd_one, normed_one = norm_forward(rows, gain_one_f, shift_one.astype(f32))
    norm_one_full = lax.all_gather(normed_one.astype(bf16), "tensor", axis=0, tiled=True)
    total_rows = norm_one_full.shape[0]
    local_heads = query_full.shape[1] // HD
    bias_key_full = jnp.pad(key_bias.astype(f32), ((0, 0), (0, HD - ROT))).reshape(-1)
    q_lin = jnp.dot(norm_one_full, query_full, preferred_element_type=f32) + bias_query.astype(
        f32
    ).reshape(-1)
    k_lin = jnp.dot(norm_one_full, key_full, preferred_element_type=f32) + bias_key_full
    v_lin = jnp.dot(norm_one_full, value_full, preferred_element_type=f32) + bias_value.astype(
        f32
    ).reshape(-1)
    angles = rope_angles(positions)
    cosine = jnp.cos(angles)[:, None, :]
    sine = jnp.sin(angles)[:, None, :]
    q_rot = turn(q_lin.reshape(total_rows, local_heads, HD), cosine, sine, 1.0).astype(bf16)
    k_rot = turn(k_lin.reshape(total_rows, local_heads, HD), cosine, sine, 1.0).astype(bf16)
    v_heads = v_lin.reshape(total_rows, local_heads, HD).astype(bf16)
    mixed, log_sums = attend_forward(q_rot, k_rot, v_heads, segments)
    mixed_low = mixed.reshape(total_rows, -1).astype(bf16)
    attended = rows + lax.psum_scatter(
        jnp.dot(mixed_low, out_full, preferred_element_type=f32),
        "tensor",
        scatter_dimension=0,
        tiled=True,
    )
    gain_two_f = gain_two.astype(f32)
    hat_two, rstd_two, normed_two = norm_forward(attended, gain_two_f, shift_two.astype(f32))
    norm_two_full = lax.all_gather(normed_two.astype(bf16), "tensor", axis=0, tiled=True)
    gate_lin = jnp.dot(norm_two_full, gate_full, preferred_element_type=f32)
    up_lin = jnp.dot(norm_two_full, up_full, preferred_element_type=f32)
    sigma = jax.nn.sigmoid(gate_lin)
    activated = gate_lin * sigma
    hidden_low = (activated * up_lin).astype(bf16)
    layer_output = (
        attended
        + lax.psum_scatter(
            jnp.dot(hidden_low, down_full, preferred_element_type=f32).astype(jnp.bfloat16),
            "tensor",
            scatter_dimension=0,
            tiled=True,
        ).astype(jnp.float32)
    ).astype(bf16)
    fresh = (
        lax.all_gather(query_weight, "dp", axis=0, tiled=True),
        lax.all_gather(key_weight, "dp", axis=0, tiled=True),
        lax.all_gather(value_weight, "dp", axis=0, tiled=True),
        lax.all_gather(out_weight, "dp", axis=1, tiled=True),
        lax.all_gather(gate_weight, "dp", axis=0, tiled=True),
        lax.all_gather(up_weight, "dp", axis=0, tiled=True),
        lax.all_gather(down_weight, "dp", axis=1, tiled=True),
        lax.all_gather(second_gain, "dp", axis=0, tiled=True),
    )
    query_back, key_back, value_back, out_back, gate_back, up_back, down_back, gain_back = fresh
    grad_full = lax.all_gather(out_grad, "tensor", axis=0, tiled=True)
    grad_hidden = jnp.einsum("sd,fd->sf", grad_full, down_back, preferred_element_type=f32)
    down_grad = jnp.einsum("sf,sd->fd", hidden_low, grad_full, preferred_element_type=f32)
    grad_gate = (grad_hidden * up_lin * sigma * (1.0 + gate_lin * (1.0 - sigma))).astype(bf16)
    grad_up = (grad_hidden * activated).astype(bf16)
    gate_grad = jnp.einsum("sd,sf->df", norm_two_full, grad_gate, preferred_element_type=f32)
    up_grad = jnp.einsum("sd,sf->df", norm_two_full, grad_up, preferred_element_type=f32)
    grad_norm_two = lax.psum_scatter(
        jnp.einsum("sf,df->sd", grad_gate, gate_back, preferred_element_type=f32)
        + jnp.einsum("sf,df->sd", grad_up, up_back, preferred_element_type=f32),
        "tensor",
        scatter_dimension=0,
        tiled=True,
    )
    gain_two_grad = jnp.sum(grad_norm_two * hat_two, axis=0)
    shift_two_grad = jnp.sum(grad_norm_two, axis=0)
    grad_attended = out_grad.astype(f32) + norm_backward(
        grad_norm_two, hat_two, rstd_two, gain_back.astype(f32)
    )
    residual_full = lax.all_gather(grad_attended.astype(bf16), "tensor", axis=0, tiled=True)
    grad_mixed = jnp.einsum(
        "sd,kd->sk", residual_full, out_back, preferred_element_type=f32
    ).astype(bf16)
    out_weight_grad = jnp.einsum("sk,sd->kd", mixed_low, residual_full, preferred_element_type=f32)
    grad_qrot, grad_krot, grad_vheads = attend_backward(
        q_rot, k_rot, v_heads, segments, log_sums, grad_mixed.reshape(total_rows, local_heads, HD)
    )
    grad_query = turn(grad_qrot, cosine, sine, -1.0).reshape(total_rows, -1)
    grad_key = turn(grad_krot, cosine, sine, -1.0).reshape(total_rows, -1)
    grad_value = grad_vheads.reshape(total_rows, -1)
    query_bias_grad = jnp.sum(grad_query, axis=0).reshape(local_heads, HD)
    key_bias_grad = jnp.sum(grad_key, axis=0).reshape(local_heads, HD)[:, :ROT]
    value_bias_grad = jnp.sum(grad_value, axis=0).reshape(local_heads, HD)
    query_low = grad_query.astype(bf16)
    key_low = grad_key.astype(bf16)
    value_low = grad_value.astype(bf16)
    query_weight_grad = jnp.einsum(
        "sd,sk->dk", norm_one_full, query_low, preferred_element_type=f32
    )
    key_weight_grad = jnp.einsum("sd,sk->dk", norm_one_full, key_low, preferred_element_type=f32)
    value_weight_grad = jnp.einsum(
        "sd,sk->dk", norm_one_full, value_low, preferred_element_type=f32
    )
    total = jnp.einsum("sk,dk->sd", query_low, query_back, preferred_element_type=f32)
    total = total + jnp.einsum("sk,dk->sd", key_low, key_back, preferred_element_type=f32)
    grad_norm_one = lax.psum_scatter(
        total + jnp.einsum("sk,dk->sd", value_low, value_back, preferred_element_type=f32),
        "tensor",
        scatter_dimension=0,
        tiled=True,
    )
    gain_one_grad = jnp.sum(grad_norm_one * hat_one, axis=0)
    shift_one_grad = jnp.sum(grad_norm_one, axis=0)
    input_grad = grad_attended + norm_backward(grad_norm_one, hat_one, rstd_one, gain_one_f)
    gate_sum, up_sum, down_sum = (
        lax.psum_scatter(gate_grad, "dp", scatter_dimension=0, tiled=True),
        lax.psum_scatter(up_grad, "dp", scatter_dimension=0, tiled=True),
        lax.psum_scatter(down_grad, "dp", scatter_dimension=1, tiled=True),
    )
    query_sum, key_sum, value_sum, out_sum, bquery_sum, bvalue_sum = (
        lax.psum_scatter(query_weight_grad, "dp", scatter_dimension=0, tiled=True),
        lax.psum_scatter(key_weight_grad, "dp", scatter_dimension=0, tiled=True),
        lax.psum_scatter(value_weight_grad, "dp", scatter_dimension=0, tiled=True),
        lax.psum_scatter(out_weight_grad, "dp", scatter_dimension=1, tiled=True),
        lax.psum_scatter(query_bias_grad, "dp", scatter_dimension=1, tiled=True),
        lax.psum_scatter(value_bias_grad, "dp", scatter_dimension=1, tiled=True),
    )
    bkey_sum = lax.psum(key_bias_grad, "dp")
    gain_one_sum, shift_one_sum, gain_two_sum, shift_two_sum = (
        lax.psum_scatter(gain_one_grad, ("dp", "tensor"), scatter_dimension=0, tiled=True),
        lax.psum_scatter(shift_one_grad, ("dp", "tensor"), scatter_dimension=0, tiled=True),
        lax.psum_scatter(gain_two_grad, ("dp", "tensor"), scatter_dimension=0, tiled=True),
        lax.psum_scatter(shift_two_grad, ("dp", "tensor"), scatter_dimension=0, tiled=True),
    )
    return (
        layer_output,
        input_grad,
        gain_one_sum,
        shift_one_sum,
        query_sum,
        key_sum,
        value_sum,
        bquery_sum,
        bkey_sum,
        bvalue_sum,
        out_sum,
        gain_two_sum,
        shift_two_sum,
        gate_sum,
        up_sum,
        down_sum,
    )


def solution(mesh):
    return jax.shard_map(
        local,
        mesh=mesh,
        in_specs=(
            P(("dp", "tensor"), None),
            P("dp"),
            P("dp"),
            P("dp"),
            P("dp"),
            P("dp", "tensor"),
            P("dp", "tensor"),
            P("dp", "tensor"),
            P("tensor", "dp"),
            P("tensor", None),
            P("tensor", "dp"),
            P("tensor", "dp"),
            P("dp"),
            P("dp"),
            P("dp", "tensor"),
            P("dp", "tensor"),
            P("tensor", "dp"),
            P(("dp", "tensor"), None),
        ),
        out_specs=(
            P(("dp", "tensor"), None),
            P(("dp", "tensor"), None),
            P(("dp", "tensor")),
            P(("dp", "tensor")),
            P("dp", "tensor"),
            P("dp", "tensor"),
            P("dp", "tensor"),
            P("tensor", "dp"),
            P("tensor", None),
            P("tensor", "dp"),
            P("tensor", "dp"),
            P(("dp", "tensor")),
            P(("dp", "tensor")),
            P("dp", "tensor"),
            P("dp", "tensor"),
            P("tensor", "dp"),
        ),
        check_vma=False,
    )
```

profile of v0, /device:TPU:0, one launch (start us, length us, event | category | flops | bytes accessed | tf_op | source)
XLA Modules:
  0.0 2123.0 jit_solution(928444203976927270)
XLA Ops:
  55.5 26.0 %all_gather.66 = bf16[8,64]{0,1:T(8,128)(2,1)S(1)} all-gather(bf16[8,8]{0,1:T(8,128)(2,1)S(1)} %copy.48), channel_id=1, replica_groups=mesh['dp'=8,'tensor'=4] {'dp'}, dimensions={1}, use_global_device_ids=true | all-gather | bytes 1152 | tf_op jit(solution)/shard_map/all_gather | solution.py:146
  81.6 26.0 %all_gather.63 = bf16[8,64]{0,1:T(8,128)(2,1)S(1)} all-gather(bf16[8,8]{0,1:T(8,128)(2,1)S(1)} %copy.46), channel_id=1, replica_groups=mesh['dp'=8,'tensor'=4] {'dp'}, dimensions={1}, use_global_device_ids=true | all-gather | bytes 1152 | tf_op jit(solution)/shard_map/all_gather | solution.py:145
  115.3 33.6 %all-gather.18.cloned.1.call-done = bf16[2048,512]{1,0:T(8,128)(2,1)} async-done(((bf16[256,512]{1,0:T(8,128)(2,1)}), bf16[2048,512]{1,0:T(8,128)(2,1)}) %all-gather.18.cloned.1.call-update) | async-done | bytes 2097168 | tf_op jit(solution)/shard_map/all_gather | solution.py:141
  157.0 41.7 %all-gather.22.cloned.1.call-done = bf16[2048,512]{1,0:T(8,128)(2,1)} async-done(((bf16[256,512]{1,0:T(8,128)(2,1)}), bf16[2048,512]{1,0:T(8,128)(2,1)}) %all-gather.22.cloned.1.call-update) | async-done | bytes 2097168 | tf_op jit(solution)/shard_map/all_gather | solution.py:143
  204.9 34.0 %while.31 = (s32[]{:T(128)}, bf16[2,512,8,64]{1,3,2,0:T(8,128)(2,1)S(1)}, f32[2,8,512]{2,1,0:T(8,128)S(1)}, s32[2]{0:T(128)S(1)}, s32[1024]{0:T(1024)S(1)}, /*in...) while((s32[]{:T(128)}, ...), condition=%wide.region_5.6_spmd, body=%wide.region_2.5_spmd.sunk | while | flops 1125643776 | bytes 56252800 | solution.py:80
  292.9 34.6 %reduce-scatter.14.cloned.1.call-done = f32[256,2048]{1,0:T(8,128)} async-done(((f32[1024,2048]{1,0:T(8,128)}), f32[256,2048]{1,0:T(8,128)}) %reduce-scatter.14.cloned.1.call-update) | async-done | bytes 2097168 | tf_op jit(solution)/shard_map/reduce_scatter | solution.py:179
  333.4 89.3 %all-gather.30.cloned.1.call-done = bf16[2048,1408]{1,0:T(8,128)(2,1)} async-done(((bf16[256,1408]{1,0:T(8,128)(2,1)}), bf16[2048,1408]{1,0:T(8,128)(2,1)}) %all-gather.30.cloned.1.call-update) | async-done | bytes 5767184 | tf_op jit(solution)/shard_map/all_gather | solution.py:152
  422.6 34.9 %all-gather.26.cloned.1.call-done = bf16[1024,2048]{1,0:T(8,128)(2,1)} async-done(((bf16[256,2048]{1,0:T(8,128)(2,1)}), bf16[1024,2048]{1,0:T(8,128)(2,1)}) %all-gather.26.cloned.1.call-update) | async-done | bytes 4194320 | tf_op jit(solution)/shard_map/all_gather | solution.py:187
  469.5 83.2 %all-gather.28.cloned.1.call-done = bf16[2048,1408]{1,0:T(8,128)(2,1)} async-done(((bf16[256,1408]{1,0:T(8,128)(2,1)}), bf16[2048,1408]{1,0:T(8,128)(2,1)}) %all-gather.28.cloned.1.call-update) | async-done | bytes 5767184 | tf_op jit(solution)/shard_map/all_gather | solution.py:151
  586.8 95.9 %all-gather.32.cloned.1.call-done = bf16[1408,2048]{1,0:T(8,128)(2,1)} async-done(((bf16[1408,256]{1,0:T(8,128)(2,1)}), bf16[1408,2048]{1,0:T(8,128)(2,1)}) %all-gather.32.cloned.1.call-update) | async-done | bytes 5767184 | tf_op jit(solution)/shard_map/all_gather | solution.py:153
  730.4 59.0 %reduce-scatter.18.cloned.1.call-done = f32[256,2048]{1,0:T(8,128)} async-done(((f32[1024,2048]{1,0:T(8,128)}), f32[256,2048]{1,0:T(8,128)}) %reduce-scatter.18.cloned.1.call-update) | async-done | bytes 2097168 | tf_op jit(solution)/shard_map/reduce_scatter | solution.py:220
  792.5 44.0 %reduce-scatter.16.cloned.1.call-done = bf16[256,2048]{1,0:T(8,128)(2,1)} async-done(((bf16[1024,2048]{1,0:T(8,128)(2,1)}), bf16[256,2048]{1,0:T(8,128)(2,1)}) %reduce-scatter.16.cloned.1.call-update) | async-done | bytes 1048592 | tf_op jit(solution)/shard_map/reduce_scatter | solution.py:195
  841.6 34.6 %all-gather.36.cloned.1.call-done = bf16[1024,2048]{1,0:T(8,128)(2,1)} async-done(((bf16[256,2048]{1,0:T(8,128)(2,1)}), bf16[1024,2048]{1,0:T(8,128)(2,1)}) %all-gather.36.cloned.1.call-update) | async-done | bytes 4194320 | tf_op jit(solution)/shard_map/all_gather | solution.py:232
  882.4 183.4 %while.32 = (s32[]{:T(128)}, f32[1024,8,64]{0,2,1:T(8,128)}, f32[1024,8,64]{0,2,1:T(8,128)S(1)}, f32[2,512,8,64]{1,0,3,2:T(2,128)}, s32[2]{0:T(128)S(1)}, /*inde...) while((s32[]{:T(128)}, f32[1024,8,64]{0,2,1:T(8,128)}, ...), condition=%wide.region_15.16_spmd.clone, body=%wide.region_13.15_spmd.clone.sunk | while | flops 2746756608 | bytes 238098896 | solution.py:112
  1019.6 24.0 %bitcast_add_fusion.4 = f32[1024,8,64]{0,2,1:T(8,128)} fusion(f32[1024,8,64]{0,2,1:T(8,128)} %get-tuple-element.566, f32[8,512,1024]{2,1,0:T(8,128)} %copy-done, f32[8,512,1024]{2,1,0:T(8,128)} %fusion.158, pred[]{:T(512)S(6)} %compare.14, bf16[1024,8,64]{0,2,1:T(8,128)(2,1)} %get-tuple-element.588, s32[]{:T(128)S(6)} %select_n.75), kind=kOutput, calls=%fused_computation.29.clone.1 | convolution fusion | flops 558896128 | bytes 71827464 | tf_op jit(solution)/shard_map/while/body/eval_jaxpr/hqk,qhd->khd/dot_general | solution.py:101
  1154.6 38.4 %all-reduce.8 = (f32[8,64]{1,0:T(8,128)S(1)}, f32[8,16]{1,0:T(8,128)}, f32[8,64]{1,0:T(8,128)S(1)}) all-reduce(f32[8,64]{1,0:T(8,128)S(1)} %fusion.61, f32[8,16]{1,0:T(8,128)S(1)} %bitcast.138, f32[8,64]{1,0:T(8,128)S(1)} %get-tuple-element.370), channel_id=11, replica_groups=mesh['dp'=8,'tensor'=4] {'dp'}, use_global_device_ids=true, to_apply=%region_27.28.clone | all-reduce | flops 1152 | bytes 9216
  1197.0 41.2 %all-reduce.7 = (f32[2048]{0:T(1024)S(1)}, f32[2048]{0:T(1024)S(1)}, f32[2048]{0:T(1024)S(1)}, f32[2048]{0:T(1024)S(1)}) all-reduce(f32[2048]{0:T(1024)S(1)} %get-tuple-element.302, f32[2048]{0:T(1024)S(1)} %get-tuple-element.307, f32[2048]{0:T(1024)S(1)} %copy-done.24, ...), channel_id=6, replica_groups=mesh['dp'=8,'tensor'=4] {'dp','tensor'}, use_global_device_ids=true, to_apply=%region_20.21.clone | all-reduce | flops 8192 | bytes 65536
  1244.3 112.0 %reduce-scatter.34.cloned.1.call-done = f32[1408,256]{1,0:T(8,128)} async-done(((f32[1408,2048]{1,0:T(8,128)}), f32[1408,256]{1,0:T(8,128)}) %reduce-scatter.34.cloned.1.call-update) | async-done | bytes 1441808 | tf_op jit(solution)/shard_map/reduce_scatter | solution.py:270
  1356.3 195.9 %reduce-scatter.32.cloned.1.call-done = f32[256,1408]{1,0:T(8,128)} async-done(((f32[2048,1408]{1,0:T(8,128)}), f32[256,1408]{1,0:T(8,128)}) %reduce-scatter.32.cloned.1.call-update) | async-done | bytes 1441808 | tf_op jit(solution)/shard_map/reduce_scatter | solution.py:269
  1552.1 195.9 %reduce-scatter.30.cloned.1.call-done = f32[256,1408]{1,0:T(8,128)} async-done(((f32[2048,1408]{1,0:T(8,128)}), f32[256,1408]{1,0:T(8,128)}) %reduce-scatter.30.cloned.1.call-update) | async-done | bytes 1441808 | tf_op jit(solution)/shard_map/reduce_scatter | solution.py:268
  1748.0 91.6 %reduce-scatter.28.cloned.1.call-done = f32[512,256]{1,0:T(8,128)} async-done(((f32[512,2048]{1,0:T(8,128)}), f32[512,256]{1,0:T(8,128)}) %reduce-scatter.28.cloned.1.call-update) | async-done | bytes 524304 | tf_op jit(solution)/shard_map/reduce_scatter | solution.py:276
  1839.7 92.2 %reduce-scatter.26.cloned.1.call-done = f32[256,512]{1,0:T(8,128)} async-done(((f32[2048,512]{1,0:T(8,128)}), f32[256,512]{1,0:T(8,128)}) %reduce-scatter.26.cloned.1.call-update) | async-done | bytes 524304 | tf_op jit(solution)/shard_map/reduce_scatter | solution.py:275
  1931.8 91.9 %reduce-scatter.24.cloned.1.call-done = f32[256,512]{1,0:T(8,128)} async-done(((f32[2048,512]{1,0:T(8,128)}), f32[256,512]{1,0:T(8,128)}) %reduce-scatter.24.cloned.1.call-update) | async-done | bytes 524304 | tf_op jit(solution)/shard_map/reduce_scatter | solution.py:274
  2023.7 92.3 %reduce-scatter.22.cloned.1.call-done = f32[256,512]{1,0:T(8,128)} async-done(((f32[2048,512]{1,0:T(8,128)}), f32[256,512]{1,0:T(8,128)}) %reduce-scatter.22.cloned.1.call-update) | async-done | bytes 524304 | tf_op jit(solution)/shard_map/reduce_scatter | solution.py:273
  (267 shorter events, 525.8 us)
Async XLA Ops:
  7.2 101.4 %all-gather.20.cloned.1.call-start = ((), (), s32[]{:S(2)}) async-start(), calls=%async_computation.13 | async-start | bytes 2359296 | tf_op jit(solution)/shard_map/all_gather | solution.py:142
  7.9 100.7 %all-gather.16.cloned.1.call-start = ((), (), s32[]{:S(2)}) async-start(), calls=%async_computation.11 | async-start | bytes 5242880 | tf_op jit(solution)/shard_map/all_gather | solution.py:160
  53.2 95.7 %all-gather.18.cloned.1.call-start = ((), (), s32[]{:S(2)}) async-start(), calls=%async_computation.12 | async-start | bytes 2359296 | tf_op jit(solution)/shard_map/all_gather | solution.py:141
  53.9 144.8 %all-gather.22.cloned.1.call-start = ((), (), s32[]{:S(2)}) async-start(), calls=%async_computation.14 | async-start | bytes 2359296 | tf_op jit(solution)/shard_map/all_gather | solution.py:143
  54.5 195.7 %all-gather.24.cloned.1.call-start = ((), (), s32[]{:S(2)}) async-start(), calls=%async_computation.15 | async-start | bytes 2359296 | tf_op jit(solution)/shard_map/all_gather | solution.py:144
  55.1 272.5 %reduce-scatter.14.cloned.1.call-start = ((), (), s32[]{:S(2)}) async-start(), calls=%async_computation.16 | async-start | bytes 10485760 | tf_op jit(solution)/shard_map/reduce_scatter | solution.py:179
  257.5 70.1 %copy-start.2 = (bf16[256,2048]{1,0:T(8,128)(2,1)S(1)}, bf16[256,2048]{1,0:T(8,128)(2,1)}, u32[]{:S(2)}) copy-start(bf16[256,2048]{1,0:T(8,128)(2,1)} %param.22) | copy-start | bytes 3145732
  257.5 165.1 %all-gather.30.cloned.1.call-start = ((), (), s32[]{:S(2)}) async-start(), calls=%async_computation.19 | async-start | bytes 6488064 | tf_op jit(solution)/shard_map/all_gather | solution.py:152
  258.3 199.3 %all-gather.26.cloned.1.call-start = ((), (), s32[]{:S(2)}) async-start(), calls=%async_computation.17 | async-start | bytes 5242880 | tf_op jit(solution)/shard_map/all_gather | solution.py:187
  331.3 221.4 %all-gather.28.cloned.1.call-start = ((), (), s32[]{:S(2)}) async-start(), calls=%async_computation.18 | async-start | bytes 6488064 | tf_op jit(solution)/shard_map/all_gather | solution.py:151
  332.0 254.8 %all-gather.34.cloned.1.call-start = ((), (), s32[]{:S(2)}) async-start(), calls=%async_computation.22 | async-start | bytes 5242880 | tf_op jit(solution)/shard_map/all_gather | solution.py:213
  332.6 350.1 %all-gather.32.cloned.1.call-start = ((), (), s32[]{:S(2)}) async-start(), calls=%async_computation.20 | async-start | bytes 6488064 | tf_op jit(solution)/shard_map/all_gather | solution.py:153
  333.3 456.1 %reduce-scatter.18.cloned.1.call-start = ((), (), s32[]{:S(2)}) async-start(), calls=%async_computation.23 | async-start | bytes 10485760 | tf_op jit(solution)/shard_map/reduce_scatter | solution.py:220
  719.3 117.2 %reduce-scatter.16.cloned.1.call-start = ((), (), s32[]{:S(2)}) async-start(), calls=%async_computation.21 | async-start | bytes 5242880 | tf_op jit(solution)/shard_map/reduce_scatter | solution.py:195
  730.3 106.2 %copy-start.8 = (bf16[256,2048]{1,0:T(8,128)(2,1)S(1)}, bf16[256,2048]{1,0:T(8,128)(2,1)}, u32[]{:S(2)}) copy-start(bf16[256,2048]{1,0:T(8,128)(2,1)} %param.39) | copy-start | bytes 3145732
  730.4 145.8 %all-gather.36.cloned.1.call-start = ((), (), s32[]{:S(2)}) async-start(), calls=%async_computation.24 | async-start | bytes 5242880 | tf_op jit(solution)/shard_map/all_gather | solution.py:232
  841.5 352.8 %reduce-scatter.20.cloned.1.call-start = ((), (), s32[]{:S(2)}) async-start(), calls=%async_computation.25 | async-start | bytes 10485760 | tf_op jit(solution)/shard_map/reduce_scatter | solution.py:258
  1086.1 270.2 %reduce-scatter.34.cloned.1.call-start = ((), (), s32[]{:S(2)}) async-start(), calls=%async_computation.32 | async-start | bytes 12976128 | tf_op jit(solution)/shard_map/reduce_scatter | solution.py:270
  1098.4 453.7 %reduce-scatter.32.cloned.1.call-start = ((), (), s32[]{:S(2)}) async-start(), calls=%async_computation.31 | async-start | bytes 12976128 | tf_op jit(solution)/shard_map/reduce_scatter | solution.py:269
  1111.5 636.5 %reduce-scatter.30.cloned.1.call-start = ((), (), s32[]{:S(2)}) async-start(), calls=%async_computation.30 | async-start | bytes 12976128 | tf_op jit(solution)/shard_map/reduce_scatter | solution.py:268
  1123.5 716.1 %reduce-scatter.28.cloned.1.call-start = ((), (), s32[]{:S(2)}) async-start(), calls=%async_computation.29 | async-start | bytes 4718592 | tf_op jit(solution)/shard_map/reduce_scatter | solution.py:276
  1130.6 801.2 %reduce-scatter.26.cloned.1.call-start = ((), (), s32[]{:S(2)}) async-start(), calls=%async_computation.28 | async-start | bytes 4718592 | tf_op jit(solution)/shard_map/reduce_scatter | solution.py:275
  1137.4 886.3 %reduce-scatter.24.cloned.1.call-start = ((), (), s32[]{:S(2)}) async-start(), calls=%async_computation.27 | async-start | bytes 4718592 | tf_op jit(solution)/shard_map/reduce_scatter | solution.py:274
  1144.2 971.8 %reduce-scatter.22.cloned.1.call-start = ((), (), s32[]{:S(2)}) async-start(), calls=%async_computation.26 | async-start | bytes 4718592 | tf_op jit(solution)/shard_map/reduce_scatter | solution.py:273
  (40 other events, 565.2 us)
Sparse Core Ops, SparseCore 0:
  10.2 52.0 all-gather.19
  64.4 33.0 all-gather.15
  99.6 49.2 all-gather.17
  150.9 47.7 all-gather.21
  200.6 49.5 all-gather.23
  257.6 69.8 reduce-scatter.13
  330.0 92.6 all-gather.29
  424.9 32.6 all-gather.25
  460.0 92.6 all-gather.27
  554.1 32.6 all-gather.33
  589.1 93.5 all-gather.31
  719.5 69.9 reduce-scatter.17
  791.9 44.5 reduce-scatter.15
  841.6 34.4 all-gather.35
  1086.2 71.6 reduce-scatter.19
  1162.0 194.2 reduce-scatter.33
  1360.3 191.8 reduce-scatter.31
  1556.2 191.8 reduce-scatter.29
  1752.2 87.3 reduce-scatter.27
  1844.1 87.6 reduce-scatter.25
  1936.0 87.6 reduce-scatter.23
  2028.3 87.6 reduce-scatter.21
where the time goes:
time: 2130 us; the launch traced here: 2120 us
  waiting for transfers between devices  1460 us (69%)
  matrix products  328 us (15%)
  blocking collectives  205 us (10%)
  local copies, waits for them, and re-layouts  69 us (3%)
  other arithmetic  40.7 us (2%)
    reduce_scatter x1, waiting for transfers between devices, local(): lax.psum_scatter(gate_grad, 'dp', scatter_dimension=0, tiled=True)  196 us
    reduce_scatter x1, waiting for transfers between devices, local(): lax.psum_scatter(up_grad, 'dp', scatter_dimension=0, tiled=True)  196 us
    reduce_scatter x1, waiting for transfers between devices, local(): lax.psum_scatter(down_grad, 'dp', scatter_dimension=1, tiled=True)  112 us
    all_gather x1, waiting for transfers between devices, local(): lax.all_gather(down_weight, 'dp', axis=1, tiled=True)  95.9 us
    reduce_scatter x1, waiting for transfers between devices, local(): lax.psum_scatter(query_weight_grad, 'dp', scatter_dimension=0, tiled=True)  92.3 us
    reduce_scatter x1, waiting for transfers between devices, local(): lax.psum_scatter(value_weight_grad, 'dp', scatter_dimension=0, tiled=True)  92.2 us
    reduce_scatter x1, waiting for transfers between devices, local(): lax.psum_scatter(key_weight_grad, 'dp', scatter_dimension=0, tiled=True)  91.9 us
    reduce_scatter x1, waiting for transfers between devices, local(): lax.psum_scatter(out_weight_grad, 'dp', scatter_dimension=1, tiled=True)  91.6 us
  transfers between devices with their start and end apart: 22, of which 19 were waited for; matrix products, arithmetic and copies ran while one was open for 8% of the time, Pallas kernels for 0%

commit v1 on v0

--- a/solution.py
+++ b/solution.py
@@ -9,6 +9,22 @@
 SEQ = 1024
 EPS = 1e-05
 NEG = -1e30
+
+
+def gather_around(x, axis, dim):
+    ways, here, step = (lax.axis_size(axis), lax.axis_index(axis), x.shape[dim])
+    dims = [n * ways if d == dim else n for d, n in enumerate(x.shape)]
+    full = lax.dynamic_update_slice_in_dim(jnp.zeros(dims, x.dtype), x, here * step, axis=dim)
+    going_up = going_down = x
+    for far in range(1, ways // 2 + 1):
+        going_up = lax.ppermute(going_up, axis, [(d, (d + 1) % ways) for d in range(ways)])
+        full = lax.dynamic_update_slice_in_dim(full, going_up, (here - far) % ways * step, axis=dim)
+        if 2 * far < ways:
+            going_down = lax.ppermute(going_down, axis, [(d, (d - 1) % ways) for d in range(ways)])
+            full = lax.dynamic_update_slice_in_dim(
+                full, going_down, (here + far) % ways * step, axis=dim
+            )
+    return full
 
 
 def rope_angles(positions):
@@ -148,7 +164,7 @@
         lax.all_gather(first_shift, "dp", axis=0, tiled=True),
     )
     gate_full, up_full, down_full, gain_two, shift_two = (
-        lax.all_gather(gate_weight, "dp", axis=0, tiled=True),
+        gather_around(gate_weight, "dp", 0),
         lax.all_gather(up_weight, "dp", axis=0, tiled=True),
         lax.all_gather(down_weight, "dp", axis=1, tiled=True),
         lax.all_gather(second_gain, "dp", axis=0, tiled=True),

time: 2130 us -> 2160 us (1.014)
    ppermute x0 -> x7, waiting for transfers between devices: none -> 113 us  [the longest x4 104 us: gather_around(): lax.ppermute(going_up, axis, [(d, (d + 1) % ways) for d in range(ways)])]
    all_gather x1, waiting for transfers between devices: 95.9 us -> 31.6 us  [local(): lax.all_gather(down_weight, 'dp', axis=1, tiled=True)]
    all_gather x1, waiting for transfers between devices: 22.5 us -> 0.01 us  [local(): grad_full = lax.all_gather(out_grad, 'tensor', axis=0, tiled=True)]
  transfers between devices with their start and end apart: 22 -> 29, of which waited for: 19 -> 23; matrix products, arithmetic and copies ran while one was open for 8% -> 10% of each run, Pallas kernels for 0% -> 0%
where the time goes in v1:
time: 2160 us; the launch traced here: 2150 us
  waiting for transfers between devices  1460 us (68%)
  matrix products  323 us (15%)
  blocking collectives  205 us (9%)
  local copies, waits for them, and re-layouts  82.7 us (4%)
  other arithmetic  40.7 us (2%)
    reduce_scatter x1, waiting for transfers between devices, local(): lax.psum_scatter(gate_grad, 'dp', scatter_dimension=0, tiled=True)  196 us
    reduce_scatter x1, waiting for transfers between devices, local(): lax.psum_scatter(up_grad, 'dp', scatter_dimension=0, tiled=True)  196 us
    reduce_scatter x1, waiting for transfers between devices, local(): lax.psum_scatter(down_grad, 'dp', scatter_dimension=1, tiled=True)  112 us
    ppermute x4, waiting for transfers between devices, gather_around(): lax.ppermute(going_up, axis, [(d, (d + 1) % ways) for d in range(ways)])  104 us
    reduce_scatter x1, waiting for transfers between devices, local(): lax.psum_scatter(query_weight_grad, 'dp', scatter_dimension=0, tiled=True)  92.3 us
    reduce_scatter x1, waiting for transfers between devices, local(): lax.psum_scatter(value_weight_grad, 'dp', scatter_dimension=0, tiled=True)  92.2 us
    reduce_scatter x1, waiting for transfers between devices, local(): lax.psum_scatter(key_weight_grad, 'dp', scatter_dimension=0, tiled=True)  91.9 us
    reduce_scatter x1, waiting for transfers between devices, local(): lax.psum_scatter(out_weight_grad, 'dp', scatter_dimension=1, tiled=True)  91.6 us
  transfers between devices with their start and end apart: 29, of which 23 were waited for; matrix products, arithmetic and copies ran while one was open for 10% of the time, Pallas kernels for 0%

profile of v1, /device:TPU:0, one launch (start us, length us, event | category | flops | bytes accessed | tf_op | source)
XLA Modules:
  0.0 2151.6 jit_solution(16382517630903046264)
XLA Ops:
  81.6 26.0 %all_gather.62 = bf16[8,64]{0,1:T(8,128)(2,1)S(1)} all-gather(bf16[8,8]{0,1:T(8,128)(2,1)S(1)} %copy.46), channel_id=1, replica_groups=mesh['dp'=8,'tensor'=4] {'dp'}, dimensions={1}, use_global_device_ids=true | all-gather | bytes 1152 | tf_op jit(solution)/shard_map/all_gather | solution.py:161
  115.3 33.6 %all-gather.18.cloned.1.call-done = bf16[2048,512]{1,0:T(8,128)(2,1)} async-done(((bf16[256,512]{1,0:T(8,128)(2,1)}), bf16[2048,512]{1,0:T(8,128)(2,1)}) %all-gather.18.cloned.1.call-update) | async-done | bytes 2097168 | tf_op jit(solution)/shard_map/all_gather | solution.py:157
  157.0 41.7 %all-gather.22.cloned.1.call-done = bf16[2048,512]{1,0:T(8,128)(2,1)} async-done(((bf16[256,512]{1,0:T(8,128)(2,1)}), bf16[2048,512]{1,0:T(8,128)(2,1)}) %all-gather.22.cloned.1.call-update) | async-done | bytes 2097168 | tf_op jit(solution)/shard_map/all_gather | solution.py:159
  204.9 34.0 %while.31 = (s32[]{:T(128)}, bf16[2,512,8,64]{1,3,2,0:T(8,128)(2,1)S(1)}, f32[2,8,512]{2,1,0:T(8,128)S(1)}, s32[2]{0:T(128)S(1)}, s32[1024]{0:T(1024)S(1)}, /*in...) while((s32[]{:T(128)}, ...), condition=%wide.region_5.6_spmd, body=%wide.region_2.5_spmd.sunk | while | flops 1125643776 | bytes 56252800 | solution.py:96
  294.4 33.1 %reduce-scatter.14.cloned.1.call-done = f32[256,2048]{1,0:T(8,128)} async-done(((f32[1024,2048]{1,0:T(8,128)}), f32[256,2048]{1,0:T(8,128)}) %reduce-scatter.14.cloned.1.call-update) | async-done | bytes 2097168 | tf_op jit(solution)/shard_map/reduce_scatter | solution.py:195
  336.1 27.9 %collective-permute-done = bf16[256,1408]{1,0:T(8,128)(2,1)} collective-permute-done((bf16[256,1408]{1,0:T(8,128)(2,1)}, bf16[256,1408]{1,0:T(8,128)(2,1)}, u32[]{:S(2)}, u32[]{:S(2)}) %collective-permute-start) | collective-permute-done | bytes 720928 | tf_op jit(solution)/shard_map/ppermute | solution.py:20
  374.5 30.0 %collective-permute-done.2 = bf16[256,1408]{1,0:T(8,128)(2,1)S(1)} collective-permute-done((bf16[256,1408]{1,0:T(8,128)(2,1)}, bf16[256,1408]{1,0:T(8,128)(2,1)S(1)}, u32[]{:S(2)}, u32[]{:S(2)}) %collective-permute-start.2) | collective-permute-done | bytes 720928 | tf_op jit(solution)/shard_map/ppermute | solution.py:20
  474.8 31.6 %all-gather.30.cloned.1.call-done = bf16[1408,2048]{1,0:T(8,128)(2,1)} async-done(((bf16[1408,256]{1,0:T(8,128)(2,1)}), bf16[1408,2048]{1,0:T(8,128)(2,1)}) %all-gather.30.cloned.1.call-update) | async-done | bytes 5767184 | tf_op jit(solution)/shard_map/all_gather | solution.py:169
  518.1 81.4 %all-gather.28.cloned.1.call-done = bf16[2048,1408]{1,0:T(8,128)(2,1)} async-done(((bf16[256,1408]{1,0:T(8,128)(2,1)}), bf16[2048,1408]{1,0:T(8,128)(2,1)}) %all-gather.28.cloned.1.call-update) | async-done | bytes 5767184 | tf_op jit(solution)/shard_map/all_gather | solution.py:168
  599.5 34.8 %all-gather.26.cloned.1.call-done = bf16[1024,2048]{1,0:T(8,128)(2,1)} async-done(((bf16[256,2048]{1,0:T(8,128)(2,1)}), bf16[1024,2048]{1,0:T(8,128)(2,1)}) %all-gather.26.cloned.1.call-update) | async-done | bytes 4194320 | tf_op jit(solution)/shard_map/all_gather | solution.py:203
  659.1 70.3 %all-gather.34.cloned.1.call-done = bf16[2048,1408]{1,0:T(8,128)(2,1)} async-done(((bf16[256,1408]{1,0:T(8,128)(2,1)}), bf16[2048,1408]{1,0:T(8,128)(2,1)}) %all-gather.34.cloned.1.call-update) | async-done | bytes 5767184 | tf_op jit(solution)/shard_map/all_gather | solution.py:223
  759.5 59.0 %reduce-scatter.18.cloned.1.call-done = f32[256,2048]{1,0:T(8,128)} async-done(((f32[1024,2048]{1,0:T(8,128)}), f32[256,2048]{1,0:T(8,128)}) %reduce-scatter.18.cloned.1.call-update) | async-done | bytes 2097168 | tf_op jit(solution)/shard_map/reduce_scatter | solution.py:236
  821.6 44.0 %reduce-scatter.16.cloned.1.call-done = bf16[256,2048]{1,0:T(8,128)(2,1)} async-done(((bf16[1024,2048]{1,0:T(8,128)(2,1)}), bf16[256,2048]{1,0:T(8,128)(2,1)}) %reduce-scatter.16.cloned.1.call-update) | async-done | bytes 1048592 | tf_op jit(solution)/shard_map/reduce_scatter | solution.py:211
  870.6 34.6 %all-gather.36.cloned.1.call-done = bf16[1024,2048]{1,0:T(8,128)(2,1)} async-done(((bf16[256,2048]{1,0:T(8,128)(2,1)}), bf16[1024,2048]{1,0:T(8,128)(2,1)}) %all-gather.36.cloned.1.call-update) | async-done | bytes 4194320 | tf_op jit(solution)/shard_map/all_gather | solution.py:248
  911.4 183.1 %while.32 = (s32[]{:T(128)}, f32[1024,8,64]{0,2,1:T(8,128)}, f32[1024,8,64]{0,2,1:T(8,128)S(1)}, f32[2,512,8,64]{1,0,3,2:T(2,128)}, s32[2]{0:T(128)S(1)}, /*inde...) while((s32[]{:T(128)}, f32[1024,8,64]{0,2,1:T(8,128)}, ...), condition=%wide.region_15.16_spmd.clone, body=%wide.region_13.15_spmd.clone.sunk | while | flops 2746756608 | bytes 238098896 | solution.py:128
  1183.3 38.5 %all-reduce.8 = (f32[8,64]{1,0:T(8,128)S(1)}, f32[8,16]{1,0:T(8,128)}, f32[8,64]{1,0:T(8,128)S(1)}) all-reduce(f32[8,64]{1,0:T(8,128)S(1)} %fusion.61, f32[8,16]{1,0:T(8,128)S(1)} %bitcast.138, f32[8,64]{1,0:T(8,128)S(1)} %get-tuple-element.370), channel_id=11, replica_groups=mesh['dp'=8,'tensor'=4] {'dp'}, use_global_device_ids=true, to_apply=%region_27.28.clone | all-reduce | flops 1152 | bytes 9216
  1225.9 41.1 %all-reduce.7 = (f32[2048]{0:T(1024)S(1)}, f32[2048]{0:T(1024)S(1)}, f32[2048]{0:T(1024)S(1)}, f32[2048]{0:T(1024)S(1)}) all-reduce(f32[2048]{0:T(1024)S(1)} %get-tuple-element.302, f32[2048]{0:T(1024)S(1)} %get-tuple-element.307, f32[2048]{0:T(1024)S(1)} %copy-done.24, ...), channel_id=6, replica_groups=mesh['dp'=8,'tensor'=4] {'dp','tensor'}, use_global_device_ids=true, to_apply=%region_20.21.clone | all-reduce | flops 8192 | bytes 65536
  1273.1 111.9 %reduce-scatter.34.cloned.1.call-done = f32[1408,256]{1,0:T(8,128)} async-done(((f32[1408,2048]{1,0:T(8,128)}), f32[1408,256]{1,0:T(8,128)}) %reduce-scatter.34.cloned.1.call-update) | async-done | bytes 1441808 | tf_op jit(solution)/shard_map/reduce_scatter | solution.py:286
  1385.0 195.8 %reduce-scatter.32.cloned.1.call-done = f32[256,1408]{1,0:T(8,128)} async-done(((f32[2048,1408]{1,0:T(8,128)}), f32[256,1408]{1,0:T(8,128)}) %reduce-scatter.32.cloned.1.call-update) | async-done | bytes 1441808 | tf_op jit(solution)/shard_map/reduce_scatter | solution.py:285
  1580.8 195.8 %reduce-scatter.30.cloned.1.call-done = f32[256,1408]{1,0:T(8,128)} async-done(((f32[2048,1408]{1,0:T(8,128)}), f32[256,1408]{1,0:T(8,128)}) %reduce-scatter.30.cloned.1.call-update) | async-done | bytes 1441808 | tf_op jit(solution)/shard_map/reduce_scatter | solution.py:284
  1776.6 91.6 %reduce-scatter.28.cloned.1.call-done = f32[512,256]{1,0:T(8,128)} async-done(((f32[512,2048]{1,0:T(8,128)}), f32[512,256]{1,0:T(8,128)}) %reduce-scatter.28.cloned.1.call-update) | async-done | bytes 524304 | tf_op jit(solution)/shard_map/reduce_scatter | solution.py:292
  1868.2 92.2 %reduce-scatter.26.cloned.1.call-done = f32[256,512]{1,0:T(8,128)} async-done(((f32[2048,512]{1,0:T(8,128)}), f32[256,512]{1,0:T(8,128)}) %reduce-scatter.26.cloned.1.call-update) | async-done | bytes 524304 | tf_op jit(solution)/shard_map/reduce_scatter | solution.py:291
  1960.4 91.9 %reduce-scatter.24.cloned.1.call-done = f32[256,512]{1,0:T(8,128)} async-done(((f32[2048,512]{1,0:T(8,128)}), f32[256,512]{1,0:T(8,128)}) %reduce-scatter.24.cloned.1.call-update) | async-done | bytes 524304 | tf_op jit(solution)/shard_map/reduce_scatter | solution.py:290
  2052.3 92.3 %reduce-scatter.22.cloned.1.call-done = f32[256,512]{1,0:T(8,128)} async-done(((f32[2048,512]{1,0:T(8,128)}), f32[256,512]{1,0:T(8,128)}) %reduce-scatter.22.cloned.1.call-update) | async-done | bytes 524304 | tf_op jit(solution)/shard_map/reduce_scatter | solution.py:289
  (294 shorter events, 633.3 us)
Async XLA Ops:
  7.2 101.4 %all-gather.20.cloned.1.call-start = ((), (), s32[]{:S(2)}) async-start(), calls=%async_computation.13 | async-start | bytes 2359296 | tf_op jit(solution)/shard_map/all_gather | solution.py:158
  7.9 100.6 %all-gather.16.cloned.1.call-start = ((), (), s32[]{:S(2)}) async-start(), calls=%async_computation.11 | async-start | bytes 5242880 | tf_op jit(solution)/shard_map/all_gather | solution.py:176
  53.2 95.7 %all-gather.18.cloned.1.call-start = ((), (), s32[]{:S(2)}) async-start(), calls=%async_computation.12 | async-start | bytes 2359296 | tf_op jit(solution)/shard_map/all_gather | solution.py:157
  53.9 144.8 %all-gather.22.cloned.1.call-start = ((), (), s32[]{:S(2)}) async-start(), calls=%async_computation.14 | async-start | bytes 2359296 | tf_op jit(solution)/shard_map/all_gather | solution.py:159
  54.5 195.7 %all-gather.24.cloned.1.call-start = ((), (), s32[]{:S(2)}) async-start(), calls=%async_computation.15 | async-start | bytes 2359296 | tf_op jit(solution)/shard_map/all_gather | solution.py:160
  55.1 272.5 %reduce-scatter.14.cloned.1.call-start = ((), (), s32[]{:S(2)}) async-start(), calls=%async_computation.16 | async-start | bytes 10485760 | tf_op jit(solution)/shard_map/reduce_scatter | solution.py:195
  257.5 217.3 %all-gather.32.cloned.1.call-start = ((), (), s32[]{:S(2)}) async-start(), calls=%async_computation.21 | async-start | bytes 5242880 | tf_op jit(solution)/shard_map/all_gather | solution.py:229
  258.3 248.1 %all-gather.30.cloned.1.call-start = ((), (), s32[]{:S(2)}) async-start(), calls=%async_computation.19 | async-start | bytes 6488064 | tf_op jit(solution)/shard_map/all_gather | solution.py:169
  259.0 340.5 %all-gather.28.cloned.1.call-start = ((), (), s32[]{:S(2)}) async-start(), calls=%async_computation.18 | async-start | bytes 6488064 | tf_op jit(solution)/shard_map/all_gather | solution.py:168
  259.7 374.5 %all-gather.26.cloned.1.call-start = ((), (), s32[]{:S(2)}) async-start(), calls=%async_computation.17 | async-start | bytes 5242880 | tf_op jit(solution)/shard_map/all_gather | solution.py:203
  331.3 398.1 %all-gather.34.cloned.1.call-start = ((), (), s32[]{:S(2)}) async-start(), calls=%async_computation.22 | async-start | bytes 6488064 | tf_op jit(solution)/shard_map/all_gather | solution.py:223
  364.0 40.5 %collective-permute-start.2 = (bf16[256,1408]{1,0:T(8,128)(2,1)}, bf16[256,1408]{1,0:T(8,128)(2,1)S(1)}, u32[]{:S(2)}, u32[]{:S(2)}) collective-permute-start(bf16[256,1408]{1,0:T(8,128)(2,1)} %collective-permute-done), channel_id=1, source_target_pairs={{0,4},{4,8},{8,12},{12,16},{16,20},{20,24},{24,28},{28,0},{1,5},{5... | collective-permute-start | bytes 2162696 | tf_op jit(solution)/shard_map/ppermute | solution.py:20
  366.5 452.0 %reduce-scatter.18.cloned.1.call-start = ((), (), s32[]{:S(2)}) async-start(), calls=%async_computation.23 | async-start | bytes 10485760 | tf_op jit(solution)/shard_map/reduce_scatter | solution.py:236
  366.7 44.3 %collective-permute-start.3 = (bf16[256,1408]{1,0:T(8,128)(2,1)}, bf16[256,1408]{1,0:T(8,128)(2,1)S(1)}, u32[]{:S(2)}, u32[]{:S(2)}) collective-permute-start(bf16[256,1408]{1,0:T(8,128)(2,1)} %collective-permute-done.1), channel_id=1, source_target_pairs={{0,28},{4,0},{8,4},{12,8},{16,12},{20,16},{24,20},{28,24},{1,29},{... | collective-permute-start | bytes 2162696 | tf_op jit(solution)/shard_map/ppermute | solution.py:23
  748.5 117.1 %reduce-scatter.16.cloned.1.call-start = ((), (), s32[]{:S(2)}) async-start(), calls=%async_computation.20 | async-start | bytes 5242880 | tf_op jit(solution)/shard_map/reduce_scatter | solution.py:211
  759.5 145.7 %all-gather.36.cloned.1.call-start = ((), (), s32[]{:S(2)}) async-start(), calls=%async_computation.24 | async-start | bytes 5242880 | tf_op jit(solution)/shard_map/all_gather | solution.py:248
  870.6 352.6 %reduce-scatter.20.cloned.1.call-start = ((), (), s32[]{:S(2)}) async-start(), calls=%async_computation.25 | async-start | bytes 10485760 | tf_op jit(solution)/shard_map/reduce_scatter | solution.py:274
  1114.9 270.0 %reduce-scatter.34.cloned.1.call-start = ((), (), s32[]{:S(2)}) async-start(), calls=%async_computation.32 | async-start | bytes 12976128 | tf_op jit(solution)/shard_map/reduce_scatter | solution.py:286
  1127.3 453.5 %reduce-scatter.32.cloned.1.call-start = ((), (), s32[]{:S(2)}) async-start(), calls=%async_computation.31 | async-start | bytes 12976128 | tf_op jit(solution)/shard_map/reduce_scatter | solution.py:285
  1140.3 636.3 %reduce-scatter.30.cloned.1.call-start = ((), (), s32[]{:S(2)}) async-start(), calls=%async_computation.30 | async-start | bytes 12976128 | tf_op jit(solution)/shard_map/reduce_scatter | solution.py:284
  1152.3 715.9 %reduce-scatter.28.cloned.1.call-start = ((), (), s32[]{:S(2)}) async-start(), calls=%async_computation.29 | async-start | bytes 4718592 | tf_op jit(solution)/shard_map/reduce_scatter | solution.py:292
  1159.4 801.0 %reduce-scatter.26.cloned.1.call-start = ((), (), s32[]{:S(2)}) async-start(), calls=%async_computation.28 | async-start | bytes 4718592 | tf_op jit(solution)/shard_map/reduce_scatter | solution.py:291
  1166.2 886.1 %reduce-scatter.24.cloned.1.call-start = ((), (), s32[]{:S(2)}) async-start(), calls=%async_computation.27 | async-start | bytes 4718592 | tf_op jit(solution)/shard_map/reduce_scatter | solution.py:290
  1173.0 971.6 %reduce-scatter.22.cloned.1.call-start = ((), (), s32[]{:S(2)}) async-start(), calls=%async_computation.26 | async-start | bytes 4718592 | tf_op jit(solution)/shard_map/reduce_scatter | solution.py:289
  (49 other events, 935.2 us)
Sparse Core Ops, SparseCore 0:
  10.2 52.0 all-gather.19
  64.4 33.0 all-gather.15
  99.6 49.2 all-gather.17
  150.9 47.7 all-gather.21
  200.6 49.5 all-gather.23
  257.6 69.8 reduce-scatter.13
  329.2 34.4 all-gather.31
  365.9 140.3 all-gather.29
  508.8 90.6 all-gather.27
  601.5 32.6 all-gather.25
  636.7 92.6 all-gather.33
  748.6 69.8 reduce-scatter.17
  821.0 44.4 reduce-scatter.15
  870.7 34.4 all-gather.35
  1115.0 71.6 reduce-scatter.19
  1190.8 194.0 reduce-scatter.33
  1389.0 191.7 reduce-scatter.31
  1584.8 191.7 reduce-scatter.29
  1780.8 87.3 reduce-scatter.27
  1872.7 87.6 reduce-scatter.25
  1964.6 87.6 reduce-scatter.23
  2056.9 87.6 reduce-scatter.21
